TPU v7x, 32 devices: a whole 2x2x4 slice. The times are simulated.
32 devices in a mesh: plane: 4 (over x, core), tm: 8 (over z, y).
Axes of the slice: x: 2, y: 2, z: 4, core: 2. Of those that a mesh axis runs over, the one named last changes fastest.
Arguments:
- coeffs: float32 [32, 3, 16, 512], P('tm', None, None, 'plane'), may hold values from -1.5 to 1.5
- radius: float32 [512], P('plane'), may hold values from 0.25 to 2
- tile_mask: int32 [4, 4, 1], P(None, 'plane'), may hold values from 0 to 1
Outputs:
- hazard: float32 [4, 512], P(None, 'plane')
All inputs are finite; a program needn't handle non-finite values.
Results may differ from a plain program's by a relative error of at most 0.0003.
Values sent between devices are 32-bit elements; how exact they have to be, the bound alone decides.
No kernel may reach another device: no remote copies, remote signals or barrier semaphores. Data moves between devices by JAX's collectives and lax.ppermute only.
A program may use at most 64 MiB of HBM per device.

v0:
```python
import functools
import math

import jax
import jax.numpy as jnp
from jax import lax
from jax.experimental import pallas as pl
from jax.experimental.pallas import tpu as pltpu
from jax.sharding import PartitionSpec as P


SAMP = 32
ROUNDS = 4
AXES = 3
GROUP = 8
KINDS = 16
VMEM = pl.BlockSpec(memory_space=pltpu.VMEM)


def thirds(value):
    first = value.astype(jnp.bfloat16).astype(jnp.float32)
    rest = value - first
    second = rest.astype(jnp.bfloat16).astype(jnp.float32)
    third = (rest - second).astype(jnp.bfloat16).astype(jnp.float32)
    return first, second, third


def basis_parts(degrees):
    shape = (SAMP, 6 * degrees)
    sample = lax.broadcasted_iota(jnp.int32, shape, 0).astype(jnp.float32)
    lane = lax.broadcasted_iota(jnp.int32, shape, 1)
    nodes = -1.0 + (2.0 * sample + 1.0) / SAMP
    degree_of = lane % degrees
    before, current = jnp.ones(shape, jnp.float32), nodes
    basis = jnp.where(degree_of == 0, before, current)
    for degree in range(2, degrees):
        before, current = current, 2.0 * nodes * current - before
        basis = jnp.where(degree_of == degree, current, basis)
    first, second, third = thirds(basis * math.sqrt(1.0 / math.log(2.0)))
    part = lane // degrees
    late = jnp.where(part == 5, third, second)
    return jnp.where((part < 2) | (part == 4), first, late).astype(jnp.bfloat16)


def position_rows(basis, coeffs_ref, window):
    columns = []
    for axis in range(AXES):
        a, b, c = (part.astype(jnp.bfloat16) for part in thirds(coeffs_ref[window, axis]))
        columns.append(jnp.concatenate([a, b, a, b, c, a], axis=0))
    stacked = jnp.concatenate(columns, axis=1)
    rows = jnp.dot(basis, stacked, preferred_element_type=jnp.float32)
    width = coeffs_ref.shape[3]
    return [rows[:, axis * width:(axis + 1) * width] for axis in range(AXES)]


def features(rows):
    found = []
    for start in range(0, SAMP, GROUP):
        high, low, length = [], [], None
        for row in rows:
            value = row[start:start + GROUP]
            top = value.astype(jnp.bfloat16).astype(jnp.float32)
            bottom = (value - top).astype(jnp.bfloat16).astype(jnp.float32)
            kept = top + bottom
            length = kept * kept if length is None else length + kept * kept
            high.append(top)
            low.append(bottom)
        found.append((high, low, list(thirds(-length))))
    return found


def facing_blocks(basis, coeffs_ref):
    one = jnp.ones((GROUP, coeffs_ref.shape[3]), jnp.float32)
    blocks = []
    for window in range(coeffs_ref.shape[0]):
        for high, low, length in features(position_rows(basis, coeffs_ref, window)):
            stack = jnp.concatenate(high + low + high + [one, one, one] + length + [0.0 * one], axis=0)
            blocks.append(stack.astype(jnp.bfloat16))
    return blocks


def own_blocks(basis, coeffs_ref, left_ref):
    one = jnp.ones((GROUP, coeffs_ref.shape[3]), jnp.float32)
    place = 0
    for window in range(coeffs_ref.shape[0]):
        for high, low, length in features(position_rows(basis, coeffs_ref, window)):
            high = [2.0 * value for value in high]
            low = [2.0 * value for value in low]
            stack = jnp.concatenate(high + high + low + length + [one, one, one, 0.0 * one], axis=0)
            left_ref[place] = stack.T.astype(jnp.bfloat16)
            place += 1


def hazard_row(left_ref, blocks, scale_ref):
    objects = scale_ref.shape[0]
    depth = GROUP * KINDS
    blank = jnp.zeros((depth, objects), jnp.bfloat16)
    lane = lax.broadcasted_iota(jnp.int32, (objects, 2 * depth), 1) % GROUP
    total = jnp.zeros((objects, objects), jnp.float32)
    for pair in range(len(blocks) // 2):
        left = jnp.concatenate([left_ref[2 * pair], left_ref[2 * pair + 1]], axis=1)
        right = jnp.concatenate([
            jnp.concatenate([blocks[2 * pair], blank], axis=1),
            jnp.concatenate([blank, blocks[2 * pair + 1]], axis=1),
        ], axis=0)
        for sample in range(GROUP):
            chosen = jnp.where(lane == sample, left, jnp.zeros_like(left))
            squared = jnp.dot(chosen, right, preferred_element_type=jnp.float32)
            scale = scale_ref[...]
            total = total + (jnp.exp2(squared[:, :objects] * scale) + jnp.exp2(squared[:, objects:] * scale))
    return lax.dot_general(
        jnp.ones((8, objects), jnp.float32), total, (((1,), (1,)), ((), ())),
        precision=lax.Precision.HIGHEST, preferred_element_type=jnp.float32,
    )


def own_kernel(
    places_of, factor, coeffs_hbm, mask_hbm, radius_ref, near_ref,
    weight_ref, left_ref, spread_ref, basis_ref, blocks_ref, coeffs_ref, mask_ref, sems,
):
    copies = [
        pltpu.make_async_copy(coeffs_hbm, coeffs_ref, sems.at[0]),
        pltpu.make_async_copy(mask_hbm, mask_ref, sems.at[1]),
    ]
    for copy in copies:
        copy.start()
    objects = coeffs_ref.shape[3]
    basis = basis_parts(coeffs_ref.shape[2])
    basis_ref[...] = basis
    spread_ref[...] = jnp.broadcast_to(radius_ref[...], spread_ref.shape).T
    for place, block in enumerate(facing_blocks(basis, near_ref)):
        blocks_ref[place] = block
    for copy in copies:
        copy.wait()
    own_blocks(basis, coeffs_ref, left_ref)
    weight_ref[...] = jnp.zeros_like(weight_ref)
    for round_no, chosen in enumerate(places_of()):
        screened = jnp.broadcast_to(mask_ref[:, round_no:round_no + 1], (1, objects)).astype(jnp.float32) * factor
        for index in range(weight_ref.shape[0]):
            weight_ref[index, round_no:round_no + 1] = jnp.where(chosen == index, screened, 0.0)


def pair_kernel(place, basis_ref, left_ref, spread_ref, coeffs_ref, radius_ref, *refs):
    *earlier, sums_ref, scale_ref = refs
    if place == 0:
        blocks = [coeffs_ref[group] for group in range(coeffs_ref.shape[0])]
    else:
        blocks = facing_blocks(basis_ref[...], coeffs_ref)
    scale_ref[...] = 1.0 / (spread_ref[...] + radius_ref[...])
    row = hazard_row(left_ref, blocks, scale_ref)
    sums_ref[...] = earlier[0][...] if earlier else jnp.zeros_like(sums_ref)
    sums_ref[place:place + 1] = row[:1]


def own_side(coeffs, mask, radius, near, partner_count, places_of, factor):
    windows, _, degrees, objects = coeffs.shape
    weight, left, spread, basis, blocks = pl.pallas_call(
        functools.partial(own_kernel, places_of, factor),
        out_shape=(
            jax.ShapeDtypeStruct((partner_count, ROUNDS, objects), jnp.float32),
            jax.ShapeDtypeStruct((windows * SAMP // GROUP, objects, GROUP * KINDS), jnp.bfloat16),
            jax.ShapeDtypeStruct((objects, objects), jnp.float32),
            jax.ShapeDtypeStruct((SAMP, 6 * degrees), jnp.bfloat16),
            jax.ShapeDtypeStruct((windows * SAMP // GROUP, GROUP * KINDS, objects), jnp.bfloat16),
        ),
        in_specs=[pl.BlockSpec(memory_space=pltpu.HBM)] * 2 + [VMEM] * 2,
        out_specs=(VMEM,) * 5,
        scratch_shapes=[
            pltpu.VMEM(coeffs.shape, coeffs.dtype),
            pltpu.VMEM(mask.shape, mask.dtype),
            pltpu.SemaphoreType.DMA((2,)),
        ],
        name="own_side",
        compiler_params=pltpu.CompilerParams(vmem_limit_bytes=16 << 20),
        cost_estimate=pl.CostEstimate(flops=10_000_000, bytes_accessed=1_000_000, transcendentals=0),
    )(
        pltpu.with_memory_space_constraint(coeffs, pltpu.HBM),
        pltpu.with_memory_space_constraint(mask, pltpu.HBM),
        radius, near,
    )
    return weight, (basis, left, spread), blocks


def pair_side(place, given, coeffs, radius, sums, partner_count):
    groups, objects, _ = given[1].shape
    windows = groups * GROUP // SAMP
    operands = (*given, coeffs, radius) + (() if sums is None else (sums,))
    return pl.pallas_call(
        functools.partial(pair_kernel, place),
        out_shape=jax.ShapeDtypeStruct((partner_count, objects), jnp.float32),
        in_specs=[VMEM] * len(operands),
        out_specs=VMEM,
        scratch_shapes=[pltpu.VMEM((objects, objects), jnp.float32)],
        name="pair_side",
        compiler_params=pltpu.CompilerParams(vmem_limit_bytes=16 << 20),
        cost_estimate=pl.CostEstimate(
            flops=windows * SAMP * 4 * GROUP * KINDS * objects * objects,
            bytes_accessed=4_000_000,
            transcendentals=windows * SAMP * objects * objects,
        ),
    )(*operands)


def direct_plan(plane_count):
    steps, places = [], []
    for round_no in range(ROUNDS):
        step = (round_no // 2 + 1) * (1 if round_no % 2 == 0 else -1) % plane_count
        if step not in steps:
            steps.append(step)
        places.append(steps.index(step))
    return [[(g, (g + step) % plane_count) for g in range(plane_count)] for step in steps], places


def rotated_places():
    odd = lax.axis_index("plane") % 2
    return [1 - odd, odd, 2, 2]


def hops(times):
    bits = times.bit_length() - 1
    rounds = [[lambda time, bit=bit: time ^ (1 << bit)] for bit in reversed(range(bits))]
    if bits % 2:
        ring = (0, 1, 3, 2)

        def turned(time, turn):
            return time & ~3 | ring[(ring.index(time & 3) + turn) % 4]

        rounds[-2:] = [[lambda time, turn=turn: turned(time, turn) for turn in (1, 3, 2)]]
    return rounds


def summed(value):
    planes, times = lax.axis_size("plane"), lax.axis_size("tm")
    if times & (times - 1) or times in (1, 2) or planes % 2:
        return lax.psum(value, "tm")

    def moved(array, hop):
        pairs = [
            (plane * times + time, (plane ^ 1) * times + hop(time))
            for plane in range(planes) for time in range(times)
        ]
        return lax.ppermute(array, ("plane", "tm"), pairs)

    for steps in hops(times):
        parts = [moved(value, hop) for hop in steps + [lambda time: time]]
        while len(parts) > 1:
            parts = [left + right for left, right in zip(parts[::2], parts[1::2])]
        value = parts[0]
    return value


def local(coeffs, radius, tile_mask):
    windows, _, _, objects = coeffs.shape
    planes, times = lax.axis_size("plane"), lax.axis_size("tm")
    mask = tile_mask.reshape(1, ROUNDS)
    row = radius[None, :]
    factor = 1.0 / (windows * times * SAMP * objects)

    def taken(value, move):
        return lax.ppermute(value, "plane", move)

    def own(near, partner_count, places_of):
        return own_side(coeffs, mask, row, near, partner_count, places_of, factor)

    if planes == 4:
        beside = [(g, g ^ 1) for g in range(4)]
        opposite = [(g, g ^ 3) for g in range(4)]
        near = taken(coeffs, beside)
        across = taken(coeffs, opposite)
        near_row = taken(row, beside)
        across_row = taken(row, opposite)
        weight, given, blocks = own(near, 3, rotated_places)
        sums = pair_side(0, given, blocks, near_row, None, 3)
        across, across_row, sums = lax.optimization_barrier((across, across_row, sums))
        relayed = taken(across, beside)
        relayed_row = taken(across_row, beside)
        sums = pair_side(1, given, across, across_row, sums, 3)
        sums = pair_side(2, given, relayed, relayed_row, sums, 3)
    else:
        moves, places = direct_plan(planes)
        others = [(lax.ppermute(coeffs, "plane", move), lax.ppermute(row, "plane", move)) for move in moves]
        weight, given, blocks = own(others[0][0], len(moves), lambda: places)
        sums = pair_side(0, given, blocks, others[0][1], None, len(moves))
        for place, other in enumerate(others[1:], 1):
            sums = pair_side(place, given, *other, sums, len(moves))
    sums = summed(sums)
    return sum(weight[place] * sums[place:place + 1] for place in range(weight.shape[0]))


def solution(mesh):
    placed = (P("tm", None, None, "plane"), P("plane"), P(None, "plane", None))
    return jax.shard_map(
        local, mesh=mesh, in_specs=placed, out_specs=P(None, "plane"), check_vma=False
    )
```

profile of v0, /device:TPU:0, one launch (start us, length us, event | category | flops | bytes accessed | tf_op | source)
XLA Modules:
  0.0 23.3 jit_solution(1109884451671833522)
XLA Ops:
  0.0 0.0 copy-start
  0.0 0.5 %collective-permute-start = (f32[4,3,16,128]{3,2,1,0:T(8,128)}, f32[4,3,16,128]{3,2,1,0:T(8,128)S(1)}, u32[]{:S(2)}, u32[]{:S(2)}) collective-permute-start(f32[4,3,16,128]{3,2,1,0:T(8,128)} %coeffs_hbm.1), channel_id=1, source_target_pairs={{0,8},{8,0},{16,24},{24,16},{1,9},{9,1},{17,25},{25,17},{2,10},{10... | collective-permute-start | bytes 294920 | tf_op jit(solution)/shard_map/ppermute | solution.py:260
  0.5 0.2 copy-done
  0.7 0.5 %collective-permute-start.3 = (f32[1,128]{1,0:T(1,128)S(1)}, f32[1,128]{1,0:T(1,128)S(1)}, u32[]{:S(2)}, u32[]{:S(2)}) collective-permute-start(f32[1,128]{1,0:T(1,128)S(1)} %bitcast.22), channel_id=1, source_target_pairs={{0,8},{8,0},{16,24},{24,16},{1,9},{9,1},{17,25},{25,17},{2,10},{10... | collective-permute-start | bytes 1544 | tf_op jit(solution)/shard_map/ppermute | solution.py:260
  1.1 2.6 %collective-permute-start.2 = (f32[1,128]{1,0:T(1,128)S(1)}, f32[1,128]{1,0:T(1,128)S(1)}, u32[]{:S(2)}, u32[]{:S(2)}) collective-permute-start(f32[1,128]{1,0:T(1,128)S(1)} %bitcast.23), channel_id=1, source_target_pairs={{0,24},{8,16},{16,8},{24,0},{1,25},{9,17},{17,9},{25,1},{2,26},{10... | collective-permute-start | bytes 1544 | tf_op jit(solution)/shard_map/ppermute | solution.py:260
  3.7 0.0 collective-permute-start.1
  3.8 0.0 collective-permute-done.near_ref
  3.8 1.3 %own_side.1 = (f32[3,4,128]{2,1,0:T(4,128)S(1)}, bf16[16,128,128]{2,1,0:T(8,128)(2,1)S(1)}, f32[128,128]{1,0:T(8,128)S(1)}, bf16[32,96]{1,0:T(8,128)(2,1)S(1)}, bf16[16,128,128]{2,1,0:T(8,128)(2,1)S(1)}) custom-call(f32[4,3,16,128]{3,2,1,0:T(8,128)} %coeffs_hbm.1, s32[1,4]{1,0:T(1,128)} %bitcast.25, f32[1,128]{1,0:T(1,128)S(1)} %bitcast.24, ...), custom_call_target="tpu_custom_call" | custom-call | flops 10000000 | bytes 1000000 | tf_op jit(solution)/shard_map/own_side/pallas_call | solution.py:157
  5.1 0.0 collective-permute-done.3.radius_ref
  5.1 1.6 %pair_side.3.refs_0_ = f32[3,128]{1,0:T(4,128)S(1)} custom-call(bf16[32,96]{1,0:T(8,128)(2,1)S(1)} %get-tuple-element.14.basis_ref, bf16[16,128,128]{2,1,0:T(8,128)(2,1)S(1)} %get-tuple-element.15.left_ref, f32[128,128]{1,0:T(8,128)S(1)} %get-tuple-element.16.spread_ref, bf16[16,128,128]{2,1,0:T(8,128)(2,1)S(1)} %get-tuple-element.17.coeffs_ref, ...), custom_call_target="tpu_custom_call" | custom-call | flops 1073741824 | bytes 4000000 | tf_op jit(solution)/shard_map/pair_side/pallas_call | solution.py:188
  6.7 0.0 collective-permute-done.2.radius_ref
  6.7 2.2 %collective-permute-done.1.coeffs_ref = f32[4,3,16,128]{3,2,1,0:T(8,128)S(1)} collective-permute-done((f32[4,3,16,128]{3,2,1,0:T(8,128)}, f32[4,3,16,128]{3,2,1,0:T(8,128)S(1)}, u32[]{:S(2)}, u32[]{:S(2)}) %collective-permute-start.1) | collective-permute-done | bytes 98336 | tf_op jit(solution)/shard_map/ppermute | solution.py:260
  8.9 0.1 collective-permute-start.4
  9.0 0.4 %collective-permute-start.5 = (f32[1,128]{1,0:T(1,128)S(1)}, f32[1,128]{1,0:T(1,128)S(1)}, u32[]{:S(2)}, u32[]{:S(2)}) collective-permute-start(f32[1,128]{1,0:T(1,128)S(1)} %collective-permute-done.2.radius_ref), channel_id=1, source_target_pairs={{0,8},{8,0},{16,24},{24,16},{1,9},{9,1},{17,25},{25,17},{2,10},{10... | collective-permute-start | bytes 1544 | tf_op jit(solution)/shard_map/ppermute | solution.py:260
  9.4 1.7 %pair_side.4.refs_0_ = f32[3,128]{1,0:T(4,128)S(1)} custom-call(bf16[32,96]{1,0:T(8,128)(2,1)S(1)} %get-tuple-element.14.basis_ref, bf16[16,128,128]{2,1,0:T(8,128)(2,1)S(1)} %get-tuple-element.15.left_ref, f32[128,128]{1,0:T(8,128)S(1)} %get-tuple-element.16.spread_ref, f32[4,3,16,128]{3,2,1,0:T(8,128)S(1)} %collective-permute-done.1.coeffs_ref, ...), custom_call_target="tpu_custom_call" | custom-call | flops 1073741824 | bytes 4000000 | tf_op jit(solution)/shard_map/pair_side/pallas_call | solution.py:188
  11.1 0.0 collective-permute-done.5.radius_ref
  11.1 0.0 collective-permute-done.4.coeffs_ref
  11.1 1.8 %pair_side.5 = f32[3,128]{1,0:T(4,128)S(1)} custom-call(bf16[32,96]{1,0:T(8,128)(2,1)S(1)} %get-tuple-element.14.basis_ref, bf16[16,128,128]{2,1,0:T(8,128)(2,1)S(1)} %get-tuple-element.15.left_ref, f32[128,128]{1,0:T(8,128)S(1)} %get-tuple-element.16.spread_ref, f32[4,3,16,128]{3,2,1,0:T(8,128)S(1)} %collective-permute-done.4.coeffs_ref, ...), custom_call_target="tpu_custom_call" | custom-call | flops 1073741824 | bytes 4000000 | tf_op jit(solution)/shard_map/pair_side/pallas_call | solution.py:188
  12.9 2.3 %collective-permute-start.6 = (f32[3,128]{1,0:T(4,128)S(1)}, f32[3,128]{1,0:T(4,128)S(1)}, u32[]{:S(2)}, u32[]{:S(2)}) collective-permute-start(f32[3,128]{1,0:T(4,128)S(1)} %pair_side.5), channel_id=1, source_target_pairs={{0,12},{1,13},{2,14},{3,15},{4,8},{5,9},{6,10},{7,11},{8,4},{9,5},... | collective-permute-start | bytes 4616 | tf_op jit(solution)/shard_map/ppermute | solution.py:242
  15.2 0.4 %collective-permute-start.7 = (f32[3,128]{1,0:T(4,128)S(1)}, f32[3,128]{1,0:T(4,128)S(1)}, u32[]{:S(2)}, u32[]{:S(2)}) collective-permute-start(f32[3,128]{1,0:T(4,128)S(1)} %pair_side.5), channel_id=1, source_target_pairs={{0,8},{1,9},{2,10},{3,11},{4,12},{5,13},{6,14},{7,15},{8,0},{9,1},... | collective-permute-start | bytes 4616 | tf_op jit(solution)/shard_map/ppermute | solution.py:242
  15.6 1.2 %collective-permute-done.6 = f32[3,128]{1,0:T(4,128)S(1)} collective-permute-done((f32[3,128]{1,0:T(4,128)S(1)}, f32[3,128]{1,0:T(4,128)S(1)}, u32[]{:S(2)}, u32[]{:S(2)}) %collective-permute-start.6) | collective-permute-done | bytes 1568 | tf_op jit(solution)/shard_map/ppermute | solution.py:242
  16.8 0.0 collective-permute-done.7
  16.8 2.3 %collective-permute-start.10 = (f32[3,128]{1,0:T(4,128)S(1)}, f32[3,128]{1,0:T(4,128)S(1)}, u32[]{:S(2)}, u32[]{:S(2)}) collective-permute-start(f32[3,128]{1,0:T(4,128)S(1)} %add.18), channel_id=1, source_target_pairs={{0,11},{1,10},{2,9},{3,8},{4,15},{5,14},{6,13},{7,12},{8,3},{9,2},... | collective-permute-start | bytes 4616 | tf_op jit(solution)/shard_map/ppermute | solution.py:242
  19.1 0.4 %collective-permute-start.11 = (f32[3,128]{1,0:T(4,128)S(1)}, f32[3,128]{1,0:T(4,128)S(1)}, u32[]{:S(2)}, u32[]{:S(2)}) collective-permute-start(f32[3,128]{1,0:T(4,128)S(1)} %add.18), channel_id=1, source_target_pairs={{0,8},{1,9},{2,10},{3,11},{4,12},{5,13},{6,14},{7,15},{8,0},{9,1},... | collective-permute-start | bytes 4616 | tf_op jit(solution)/shard_map/ppermute | solution.py:242
  19.4 0.2 collective-permute-start.8
  19.7 1.5 %collective-permute-start.9 = (f32[3,128]{1,0:T(4,128)S(1)}, f32[3,128]{1,0:T(4,128)S(1)}, u32[]{:S(2)}, u32[]{:S(2)}) collective-permute-start(f32[3,128]{1,0:T(4,128)S(1)} %add.18), channel_id=1, source_target_pairs={{0,10},{1,8},{2,11},{3,9},{4,14},{5,12},{6,15},{7,13},{8,2},{9,0},... | collective-permute-start | bytes 4616 | tf_op jit(solution)/shard_map/ppermute | solution.py:242
  21.2 0.0 collective-permute-done.10
  21.2 0.0 collective-permute-done.11
  21.2 1.3 %collective-permute-done.8 = f32[3,128]{1,0:T(4,128)S(1)} collective-permute-done((f32[3,128]{1,0:T(4,128)S(1)}, f32[3,128]{1,0:T(4,128)S(1)}, u32[]{:S(2)}, u32[]{:S(2)}) %collective-permute-start.8) | collective-permute-done | bytes 1568 | tf_op jit(solution)/shard_map/ppermute | solution.py:242
  22.5 0.2 collective-permute-done.9
  22.7 0.6 %fusion = f32[4,128]{1,0:T(4,128)} fusion(f32[3,4,128]{2,1,0:T(4,128)S(1)} %get-tuple-element.13, f32[128]{0:T(128)S(1)} %get-tuple-element.22, f32[128]{0:T(128)S(1)} %get-tuple-element.23, f32[128]{0:T(128)S(1)} %get-tuple-element.21), kind=kLoop, calls=%fused_computation.1 | loop fusion | flops 2560 | bytes 9728 | tf_op jit(solution)/shard_map/add | solution.py:287
  (3 shorter events, 0.0 us)
Async XLA Ops:
  0.0 0.7 %copy-start = (f32[128]{0:T(128)S(1)}, f32[128]{0:T(128)}, u32[]{:S(2)}) copy-start(f32[128]{0:T(128)} %param.4) | copy-start | bytes 1540
  0.0 3.8 %collective-permute-start = (f32[4,3,16,128]{3,2,1,0:T(8,128)}, f32[4,3,16,128]{3,2,1,0:T(8,128)S(1)}, u32[]{:S(2)}, u32[]{:S(2)}) collective-permute-start(f32[4,3,16,128]{3,2,1,0:T(8,128)} %coeffs_hbm.1), channel_id=1, source_target_pairs={{0,8},{8,0},{16,24},{24,16},{1,9},{9,1},{17,25},{25,17},{2,10},{10... | collective-permute-start | bytes 294920 | tf_op jit(solution)/shard_map/ppermute | solution.py:260
  0.7 4.4 %collective-permute-start.3 = (f32[1,128]{1,0:T(1,128)S(1)}, f32[1,128]{1,0:T(1,128)S(1)}, u32[]{:S(2)}, u32[]{:S(2)}) collective-permute-start(f32[1,128]{1,0:T(1,128)S(1)} %bitcast.22), channel_id=1, source_target_pairs={{0,8},{8,0},{16,24},{24,16},{1,9},{9,1},{17,25},{25,17},{2,10},{10... | collective-permute-start | bytes 1544 | tf_op jit(solution)/shard_map/ppermute | solution.py:260
  1.1 5.5 %collective-permute-start.2 = (f32[1,128]{1,0:T(1,128)S(1)}, f32[1,128]{1,0:T(1,128)S(1)}, u32[]{:S(2)}, u32[]{:S(2)}) collective-permute-start(f32[1,128]{1,0:T(1,128)S(1)} %bitcast.23), channel_id=1, source_target_pairs={{0,24},{8,16},{16,8},{24,0},{1,25},{9,17},{17,9},{25,1},{2,26},{10... | collective-permute-start | bytes 1544 | tf_op jit(solution)/shard_map/ppermute | solution.py:260
  3.7 5.1 %collective-permute-start.1 = (f32[4,3,16,128]{3,2,1,0:T(8,128)}, f32[4,3,16,128]{3,2,1,0:T(8,128)S(1)}, u32[]{:S(2)}, u32[]{:S(2)}) collective-permute-start(f32[4,3,16,128]{3,2,1,0:T(8,128)} %coeffs_hbm.1), channel_id=1, source_target_pairs={{0,24},{8,16},{16,8},{24,0},{1,25},{9,17},{17,9},{25,1},{2,26},{10... | collective-permute-start | bytes 294920 | tf_op jit(solution)/shard_map/ppermute | solution.py:260
  8.9 2.2 %collective-permute-start.4 = (f32[4,3,16,128]{3,2,1,0:T(8,128)S(1)}, f32[4,3,16,128]{3,2,1,0:T(8,128)S(1)}, u32[]{:S(2)}, u32[]{:S(2)}) collective-permute-start(f32[4,3,16,128]{3,2,1,0:T(8,128)S(1)} %collective-permute-done.1.coeffs_ref), channel_id=1, source_target_pairs={{0,8},{8,0},{16,24},{24,16},{1,9},{9,1},{17,25},{25,17},{2,10},{10... | collective-permute-start | bytes 294920 | tf_op jit(solution)/shard_map/ppermute | solution.py:260
  9.0 2.1 %collective-permute-start.5 = (f32[1,128]{1,0:T(1,128)S(1)}, f32[1,128]{1,0:T(1,128)S(1)}, u32[]{:S(2)}, u32[]{:S(2)}) collective-permute-start(f32[1,128]{1,0:T(1,128)S(1)} %collective-permute-done.2.radius_ref), channel_id=1, source_target_pairs={{0,8},{8,0},{16,24},{24,16},{1,9},{9,1},{17,25},{25,17},{2,10},{10... | collective-permute-start | bytes 1544 | tf_op jit(solution)/shard_map/ppermute | solution.py:260
  12.9 3.9 %collective-permute-start.6 = (f32[3,128]{1,0:T(4,128)S(1)}, f32[3,128]{1,0:T(4,128)S(1)}, u32[]{:S(2)}, u32[]{:S(2)}) collective-permute-start(f32[3,128]{1,0:T(4,128)S(1)} %pair_side.5), channel_id=1, source_target_pairs={{0,12},{1,13},{2,14},{3,15},{4,8},{5,9},{6,10},{7,11},{8,4},{9,5},... | collective-permute-start | bytes 4616 | tf_op jit(solution)/shard_map/ppermute | solution.py:242
  15.2 1.6 %collective-permute-start.7 = (f32[3,128]{1,0:T(4,128)S(1)}, f32[3,128]{1,0:T(4,128)S(1)}, u32[]{:S(2)}, u32[]{:S(2)}) collective-permute-start(f32[3,128]{1,0:T(4,128)S(1)} %pair_side.5), channel_id=1, source_target_pairs={{0,8},{1,9},{2,10},{3,11},{4,12},{5,13},{6,14},{7,15},{8,0},{9,1},... | collective-permute-start | bytes 4616 | tf_op jit(solution)/shard_map/ppermute | solution.py:242
  16.8 4.4 %collective-permute-start.10 = (f32[3,128]{1,0:T(4,128)S(1)}, f32[3,128]{1,0:T(4,128)S(1)}, u32[]{:S(2)}, u32[]{:S(2)}) collective-permute-start(f32[3,128]{1,0:T(4,128)S(1)} %add.18), channel_id=1, source_target_pairs={{0,11},{1,10},{2,9},{3,8},{4,15},{5,14},{6,13},{7,12},{8,3},{9,2},... | collective-permute-start | bytes 4616 | tf_op jit(solution)/shard_map/ppermute | solution.py:242
  19.1 2.1 %collective-permute-start.11 = (f32[3,128]{1,0:T(4,128)S(1)}, f32[3,128]{1,0:T(4,128)S(1)}, u32[]{:S(2)}, u32[]{:S(2)}) collective-permute-start(f32[3,128]{1,0:T(4,128)S(1)} %add.18), channel_id=1, source_target_pairs={{0,8},{1,9},{2,10},{3,11},{4,12},{5,13},{6,14},{7,15},{8,0},{9,1},... | collective-permute-start | bytes 4616 | tf_op jit(solution)/shard_map/ppermute | solution.py:242
  19.4 3.0 %collective-permute-start.8 = (f32[3,128]{1,0:T(4,128)S(1)}, f32[3,128]{1,0:T(4,128)S(1)}, u32[]{:S(2)}, u32[]{:S(2)}) collective-permute-start(f32[3,128]{1,0:T(4,128)S(1)} %add.18), channel_id=1, source_target_pairs={{0,9},{1,11},{2,8},{3,10},{4,13},{5,15},{6,12},{7,14},{8,1},{9,3},... | collective-permute-start | bytes 4616 | tf_op jit(solution)/shard_map/ppermute | solution.py:242
  19.7 3.0 %collective-permute-start.9 = (f32[3,128]{1,0:T(4,128)S(1)}, f32[3,128]{1,0:T(4,128)S(1)}, u32[]{:S(2)}, u32[]{:S(2)}) collective-permute-start(f32[3,128]{1,0:T(4,128)S(1)} %add.18), channel_id=1, source_target_pairs={{0,10},{1,8},{2,11},{3,9},{4,14},{5,12},{6,15},{7,13},{8,2},{9,0},... | collective-permute-start | bytes 4616 | tf_op jit(solution)/shard_map/ppermute | solution.py:242
where the time goes:
time: 23.4 us; the launch traced here: 23.3 us
  starting transfers between devices  11.3 us (48%)
  Pallas kernels  6.37 us (27%)
  waiting for transfers between devices  4.87 us (21%)
  other arithmetic  0.59 us (3%)
    ppermute x6, starting transfers between devices, moved(): return lax.ppermute(array, ('plane', 'tm'), pairs)  7.13 us
    pallas_call x3, Pallas kernels, pair_side(): pl.pallas_call(functools.partial(pair_kernel, place), out_shape=jax.Shape...  5.06 us
    ppermute x6, starting transfers between devices, taken(): return lax.ppermute(value, 'plane', move)  4.12 us
    ppermute x6, waiting for transfers between devices, moved(): return lax.ppermute(array, ('plane', 'tm'), pairs)  2.7 us
    ppermute x6, waiting for transfers between devices, taken(): return lax.ppermute(value, 'plane', move)  2.17 us
    pallas_call x1, Pallas kernels, own_side(): pl.pallas_call(functools.partial(own_kernel, places_of, factor), out_shap...  1.32 us
    add x1, other arithmetic, local(): sum((weight[place] * sums[place:place + 1] for place in range(weight.shap...  0.59 us
  transfers between devices with their start and end apart: 12, of which 4 were waited for; matrix products, arithmetic and copies ran while one was open for 0% of the time, Pallas kernels for 20%

commit v1 on v0

--- a/solution.py
+++ b/solution.py
@@ -65,7 +65,7 @@
             length = kept * kept if length is None else length + kept * kept
             high.append(top)
             low.append(bottom)
-        found.append((high, low, list(thirds(-length))))
+        found.append((high, low, list(thirds(-length))[:2]))
     return found
 
 
@@ -74,7 +74,7 @@
     blocks = []
     for window in range(coeffs_ref.shape[0]):
         for high, low, length in features(position_rows(basis, coeffs_ref, window)):
-            stack = jnp.concatenate(high + low + high + [one, one, one] + length + [0.0 * one], axis=0)
+            stack = jnp.concatenate(high + low + high + low + [one, one] + length, axis=0)
             blocks.append(stack.astype(jnp.bfloat16))
     return blocks
 
@@ -86,7 +86,7 @@
         for high, low, length in features(position_rows(basis, coeffs_ref, window)):
             high = [2.0 * value for value in high]
             low = [2.0 * value for value in low]
-            stack = jnp.concatenate(high + high + low + length + [one, one, one, 0.0 * one], axis=0)
+            stack = jnp.concatenate(high + high + low + low + length + [one, one], axis=0)
             left_ref[place] = stack.T.astype(jnp.bfloat16)
             place += 1
 

time: 23.4 us -> 23.4 us (level)
  no operation moved by 1% of the time
where the time goes in v1:
time: 23.4 us; the launch traced here: 23.3 us
  starting transfers between devices  11.2 us (48%)
  Pallas kernels  6.39 us (27%)
  waiting for transfers between devices  4.84 us (21%)
  other arithmetic  0.59 us (3%)
    ppermute x6, starting transfers between devices, moved(): return lax.ppermute(array, ('plane', 'tm'), pairs)  7.13 us
    pallas_call x3, Pallas kernels, pair_side(): pl.pallas_call(functools.partial(pair_kernel, place), out_shape=jax.Shape...  5.05 us
    ppermute x6, starting transfers between devices, taken(): return lax.ppermute(value, 'plane', move)  4.12 us
    ppermute x6, waiting for transfers between devices, moved(): return lax.ppermute(array, ('plane', 'tm'), pairs)  2.7 us
    ppermute x6, waiting for transfers between devices, taken(): return lax.ppermute(value, 'plane', move)  2.14 us
    pallas_call x1, Pallas kernels, own_side(): pl.pallas_call(functools.partial(own_kernel, places_of, factor), out_shap...  1.35 us
    add x1, other arithmetic, local(): sum((weight[place] * sums[place:place + 1] for place in range(weight.shap...  0.59 us
  transfers between devices with their start and end apart: 12, of which 4 were waited for; matrix products, arithmetic and copies ran while one was open for 0% of the time, Pallas kernels for 20%

profile of v1, /device:TPU:0, one launch (start us, length us, event | category | flops | bytes accessed | tf_op | source)
XLA Modules:
  0.0 23.3 jit_solution(11361319409342934291)
XLA Ops:
  0.0 0.0 copy-start
  0.0 0.5 %collective-permute-start = (f32[4,3,16,128]{3,2,1,0:T(8,128)}, f32[4,3,16,128]{3,2,1,0:T(8,128)S(1)}, u32[]{:S(2)}, u32[]{:S(2)}) collective-permute-start(f32[4,3,16,128]{3,2,1,0:T(8,128)} %coeffs_hbm.1), channel_id=1, source_target_pairs={{0,8},{8,0},{16,24},{24,16},{1,9},{9,1},{17,25},{25,17},{2,10},{10... | collective-permute-start | bytes 294920 | tf_op jit(solution)/shard_map/ppermute | solution.py:260
  0.5 0.2 copy-done
  0.7 0.5 %collective-permute-start.3 = (f32[1,128]{1,0:T(1,128)S(1)}, f32[1,128]{1,0:T(1,128)S(1)}, u32[]{:S(2)}, u32[]{:S(2)}) collective-permute-start(f32[1,128]{1,0:T(1,128)S(1)} %bitcast.22), channel_id=1, source_target_pairs={{0,8},{8,0},{16,24},{24,16},{1,9},{9,1},{17,25},{25,17},{2,10},{10... | collective-permute-start | bytes 1544 | tf_op jit(solution)/shard_map/ppermute | solution.py:260
  1.1 2.6 %collective-permute-start.2 = (f32[1,128]{1,0:T(1,128)S(1)}, f32[1,128]{1,0:T(1,128)S(1)}, u32[]{:S(2)}, u32[]{:S(2)}) collective-permute-start(f32[1,128]{1,0:T(1,128)S(1)} %bitcast.23), channel_id=1, source_target_pairs={{0,24},{8,16},{16,8},{24,0},{1,25},{9,17},{17,9},{25,1},{2,26},{10... | collective-permute-start | bytes 1544 | tf_op jit(solution)/shard_map/ppermute | solution.py:260
  3.7 0.0 collective-permute-start.1
  3.8 0.0 collective-permute-done.near_ref
  3.8 1.3 %own_side.1 = (f32[3,4,128]{2,1,0:T(4,128)S(1)}, bf16[16,128,128]{2,1,0:T(8,128)(2,1)S(1)}, f32[128,128]{1,0:T(8,128)S(1)}, bf16[32,96]{1,0:T(8,128)(2,1)S(1)}, bf16[16,128,128]{2,1,0:T(8,128)(2,1)S(1)}) custom-call(f32[4,3,16,128]{3,2,1,0:T(8,128)} %coeffs_hbm.1, s32[1,4]{1,0:T(1,128)} %bitcast.25, f32[1,128]{1,0:T(1,128)S(1)} %bitcast.24, ...), custom_call_target="tpu_custom_call" | custom-call | flops 10000000 | bytes 1000000 | tf_op jit(solution)/shard_map/own_side/pallas_call | solution.py:157
  5.1 0.0 collective-permute-done.3.radius_ref
  5.1 1.6 %pair_side.3.refs_0_ = f32[3,128]{1,0:T(4,128)S(1)} custom-call(bf16[32,96]{1,0:T(8,128)(2,1)S(1)} %get-tuple-element.14.basis_ref, bf16[16,128,128]{2,1,0:T(8,128)(2,1)S(1)} %get-tuple-element.15.left_ref, f32[128,128]{1,0:T(8,128)S(1)} %get-tuple-element.16.spread_ref, bf16[16,128,128]{2,1,0:T(8,128)(2,1)S(1)} %get-tuple-element.17.coeffs_ref, ...), custom_call_target="tpu_custom_call" | custom-call | flops 1073741824 | bytes 4000000 | tf_op jit(solution)/shard_map/pair_side/pallas_call | solution.py:188
  6.7 0.0 collective-permute-done.2.radius_ref
  6.7 2.1 %collective-permute-done.1.coeffs_ref = f32[4,3,16,128]{3,2,1,0:T(8,128)S(1)} collective-permute-done((f32[4,3,16,128]{3,2,1,0:T(8,128)}, f32[4,3,16,128]{3,2,1,0:T(8,128)S(1)}, u32[]{:S(2)}, u32[]{:S(2)}) %collective-permute-start.1) | collective-permute-done | bytes 98336 | tf_op jit(solution)/shard_map/ppermute | solution.py:260
  8.9 0.1 collective-permute-start.4
  9.0 0.4 %collective-permute-start.5 = (f32[1,128]{1,0:T(1,128)S(1)}, f32[1,128]{1,0:T(1,128)S(1)}, u32[]{:S(2)}, u32[]{:S(2)}) collective-permute-start(f32[1,128]{1,0:T(1,128)S(1)} %collective-permute-done.2.radius_ref), channel_id=1, source_target_pairs={{0,8},{8,0},{16,24},{24,16},{1,9},{9,1},{17,25},{25,17},{2,10},{10... | collective-permute-start | bytes 1544 | tf_op jit(solution)/shard_map/ppermute | solution.py:260
  9.4 1.7 %pair_side.4.refs_0_ = f32[3,128]{1,0:T(4,128)S(1)} custom-call(bf16[32,96]{1,0:T(8,128)(2,1)S(1)} %get-tuple-element.14.basis_ref, bf16[16,128,128]{2,1,0:T(8,128)(2,1)S(1)} %get-tuple-element.15.left_ref, f32[128,128]{1,0:T(8,128)S(1)} %get-tuple-element.16.spread_ref, f32[4,3,16,128]{3,2,1,0:T(8,128)S(1)} %collective-permute-done.1.coeffs_ref, ...), custom_call_target="tpu_custom_call" | custom-call | flops 1073741824 | bytes 4000000 | tf_op jit(solution)/shard_map/pair_side/pallas_call | solution.py:188
  11.1 0.0 collective-permute-done.5.radius_ref
  11.1 0.0 collective-permute-done.4.coeffs_ref
  11.1 1.7 %pair_side.5 = f32[3,128]{1,0:T(4,128)S(1)} custom-call(bf16[32,96]{1,0:T(8,128)(2,1)S(1)} %get-tuple-element.14.basis_ref, bf16[16,128,128]{2,1,0:T(8,128)(2,1)S(1)} %get-tuple-element.15.left_ref, f32[128,128]{1,0:T(8,128)S(1)} %get-tuple-element.16.spread_ref, f32[4,3,16,128]{3,2,1,0:T(8,128)S(1)} %collective-permute-done.4.coeffs_ref, ...), custom_call_target="tpu_custom_call" | custom-call | flops 1073741824 | bytes 4000000 | tf_op jit(solution)/shard_map/pair_side/pallas_call | solution.py:188
  12.8 2.3 %collective-permute-start.6 = (f32[3,128]{1,0:T(4,128)S(1)}, f32[3,128]{1,0:T(4,128)S(1)}, u32[]{:S(2)}, u32[]{:S(2)}) collective-permute-start(f32[3,128]{1,0:T(4,128)S(1)} %pair_side.5), channel_id=1, source_target_pairs={{0,12},{1,13},{2,14},{3,15},{4,8},{5,9},{6,10},{7,11},{8,4},{9,5},... | collective-permute-start | bytes 4616 | tf_op jit(solution)/shard_map/ppermute | solution.py:242
  15.2 0.4 %collective-permute-start.7 = (f32[3,128]{1,0:T(4,128)S(1)}, f32[3,128]{1,0:T(4,128)S(1)}, u32[]{:S(2)}, u32[]{:S(2)}) collective-permute-start(f32[3,128]{1,0:T(4,128)S(1)} %pair_side.5), channel_id=1, source_target_pairs={{0,8},{1,9},{2,10},{3,11},{4,12},{5,13},{6,14},{7,15},{8,0},{9,1},... | collective-permute-start | bytes 4616 | tf_op jit(solution)/shard_map/ppermute | solution.py:242
  15.6 1.2 %collective-permute-done.6 = f32[3,128]{1,0:T(4,128)S(1)} collective-permute-done((f32[3,128]{1,0:T(4,128)S(1)}, f32[3,128]{1,0:T(4,128)S(1)}, u32[]{:S(2)}, u32[]{:S(2)}) %collective-permute-start.6) | collective-permute-done | bytes 1568 | tf_op jit(solution)/shard_map/ppermute | solution.py:242
  16.8 0.0 collective-permute-done.7
  16.8 2.3 %collective-permute-start.10 = (f32[3,128]{1,0:T(4,128)S(1)}, f32[3,128]{1,0:T(4,128)S(1)}, u32[]{:S(2)}, u32[]{:S(2)}) collective-permute-start(f32[3,128]{1,0:T(4,128)S(1)} %add.18), channel_id=1, source_target_pairs={{0,11},{1,10},{2,9},{3,8},{4,15},{5,14},{6,13},{7,12},{8,3},{9,2},... | collective-permute-start | bytes 4616 | tf_op jit(solution)/shard_map/ppermute | solution.py:242
  19.0 0.4 %collective-permute-start.11 = (f32[3,128]{1,0:T(4,128)S(1)}, f32[3,128]{1,0:T(4,128)S(1)}, u32[]{:S(2)}, u32[]{:S(2)}) collective-permute-start(f32[3,128]{1,0:T(4,128)S(1)} %add.18), channel_id=1, source_target_pairs={{0,8},{1,9},{2,10},{3,11},{4,12},{5,13},{6,14},{7,15},{8,0},{9,1},... | collective-permute-start | bytes 4616 | tf_op jit(solution)/shard_map/ppermute | solution.py:242
  19.4 0.2 collective-permute-start.8
  19.7 1.5 %collective-permute-start.9 = (f32[3,128]{1,0:T(4,128)S(1)}, f32[3,128]{1,0:T(4,128)S(1)}, u32[]{:S(2)}, u32[]{:S(2)}) collective-permute-start(f32[3,128]{1,0:T(4,128)S(1)} %add.18), channel_id=1, source_target_pairs={{0,10},{1,8},{2,11},{3,9},{4,14},{5,12},{6,15},{7,13},{8,2},{9,0},... | collective-permute-start | bytes 4616 | tf_op jit(solution)/shard_map/ppermute | solution.py:242
  21.2 0.0 collective-permute-done.10
  21.2 0.0 collective-permute-done.11
  21.2 1.3 %collective-permute-done.8 = f32[3,128]{1,0:T(4,128)S(1)} collective-permute-done((f32[3,128]{1,0:T(4,128)S(1)}, f32[3,128]{1,0:T(4,128)S(1)}, u32[]{:S(2)}, u32[]{:S(2)}) %collective-permute-start.8) | collective-permute-done | bytes 1568 | tf_op jit(solution)/shard_map/ppermute | solution.py:242
  22.4 0.2 collective-permute-done.9
  22.7 0.6 %fusion = f32[4,128]{1,0:T(4,128)} fusion(f32[3,4,128]{2,1,0:T(4,128)S(1)} %get-tuple-element.13, f32[128]{0:T(128)S(1)} %get-tuple-element.22, f32[128]{0:T(128)S(1)} %get-tuple-element.23, f32[128]{0:T(128)S(1)} %get-tuple-element.21), kind=kLoop, calls=%fused_computation.1 | loop fusion | flops 2560 | bytes 9728 | tf_op jit(solution)/shard_map/add | solution.py:287
  (3 shorter events, 0.0 us)
Async XLA Ops:
  0.0 0.7 %copy-start = (f32[128]{0:T(128)S(1)}, f32[128]{0:T(128)}, u32[]{:S(2)}) copy-start(f32[128]{0:T(128)} %param.4) | copy-start | bytes 1540
  0.0 3.8 %collective-permute-start = (f32[4,3,16,128]{3,2,1,0:T(8,128)}, f32[4,3,16,128]{3,2,1,0:T(8,128)S(1)}, u32[]{:S(2)}, u32[]{:S(2)}) collective-permute-start(f32[4,3,16,128]{3,2,1,0:T(8,128)} %coeffs_hbm.1), channel_id=1, source_target_pairs={{0,8},{8,0},{16,24},{24,16},{1,9},{9,1},{17,25},{25,17},{2,10},{10... | collective-permute-start | bytes 294920 | tf_op jit(solution)/shard_map/ppermute | solution.py:260
  0.7 4.5 %collective-permute-start.3 = (f32[1,128]{1,0:T(1,128)S(1)}, f32[1,128]{1,0:T(1,128)S(1)}, u32[]{:S(2)}, u32[]{:S(2)}) collective-permute-start(f32[1,128]{1,0:T(1,128)S(1)} %bitcast.22), channel_id=1, source_target_pairs={{0,8},{8,0},{16,24},{24,16},{1,9},{9,1},{17,25},{25,17},{2,10},{10... | collective-permute-start | bytes 1544 | tf_op jit(solution)/shard_map/ppermute | solution.py:260
  1.1 5.6 %collective-permute-start.2 = (f32[1,128]{1,0:T(1,128)S(1)}, f32[1,128]{1,0:T(1,128)S(1)}, u32[]{:S(2)}, u32[]{:S(2)}) collective-permute-start(f32[1,128]{1,0:T(1,128)S(1)} %bitcast.23), channel_id=1, source_target_pairs={{0,24},{8,16},{16,8},{24,0},{1,25},{9,17},{17,9},{25,1},{2,26},{10... | collective-permute-start | bytes 1544 | tf_op jit(solution)/shard_map/ppermute | solution.py:260
  3.7 5.1 %collective-permute-start.1 = (f32[4,3,16,128]{3,2,1,0:T(8,128)}, f32[4,3,16,128]{3,2,1,0:T(8,128)S(1)}, u32[]{:S(2)}, u32[]{:S(2)}) collective-permute-start(f32[4,3,16,128]{3,2,1,0:T(8,128)} %coeffs_hbm.1), channel_id=1, source_target_pairs={{0,24},{8,16},{16,8},{24,0},{1,25},{9,17},{17,9},{25,1},{2,26},{10... | collective-permute-start | bytes 294920 | tf_op jit(solution)/shard_map/ppermute | solution.py:260
  8.9 2.2 %collective-permute-start.4 = (f32[4,3,16,128]{3,2,1,0:T(8,128)S(1)}, f32[4,3,16,128]{3,2,1,0:T(8,128)S(1)}, u32[]{:S(2)}, u32[]{:S(2)}) collective-permute-start(f32[4,3,16,128]{3,2,1,0:T(8,128)S(1)} %collective-permute-done.1.coeffs_ref), channel_id=1, source_target_pairs={{0,8},{8,0},{16,24},{24,16},{1,9},{9,1},{17,25},{25,17},{2,10},{10... | collective-permute-start | bytes 294920 | tf_op jit(solution)/shard_map/ppermute | solution.py:260
  9.0 2.1 %collective-permute-start.5 = (f32[1,128]{1,0:T(1,128)S(1)}, f32[1,128]{1,0:T(1,128)S(1)}, u32[]{:S(2)}, u32[]{:S(2)}) collective-permute-start(f32[1,128]{1,0:T(1,128)S(1)} %collective-permute-done.2.radius_ref), channel_id=1, source_target_pairs={{0,8},{8,0},{16,24},{24,16},{1,9},{9,1},{17,25},{25,17},{2,10},{10... | collective-permute-start | bytes 1544 | tf_op jit(solution)/shard_map/ppermute | solution.py:260
  12.8 3.9 %collective-permute-start.6 = (f32[3,128]{1,0:T(4,128)S(1)}, f32[3,128]{1,0:T(4,128)S(1)}, u32[]{:S(2)}, u32[]{:S(2)}) collective-permute-start(f32[3,128]{1,0:T(4,128)S(1)} %pair_side.5), channel_id=1, source_target_pairs={{0,12},{1,13},{2,14},{3,15},{4,8},{5,9},{6,10},{7,11},{8,4},{9,5},... | collective-permute-start | bytes 4616 | tf_op jit(solution)/shard_map/ppermute | solution.py:242
  15.2 1.6 %collective-permute-start.7 = (f32[3,128]{1,0:T(4,128)S(1)}, f32[3,128]{1,0:T(4,128)S(1)}, u32[]{:S(2)}, u32[]{:S(2)}) collective-permute-start(f32[3,128]{1,0:T(4,128)S(1)} %pair_side.5), channel_id=1, source_target_pairs={{0,8},{1,9},{2,10},{3,11},{4,12},{5,13},{6,14},{7,15},{8,0},{9,1},... | collective-permute-start | bytes 4616 | tf_op jit(solution)/shard_map/ppermute | solution.py:242
  16.8 4.4 %collective-permute-start.10 = (f32[3,128]{1,0:T(4,128)S(1)}, f32[3,128]{1,0:T(4,128)S(1)}, u32[]{:S(2)}, u32[]{:S(2)}) collective-permute-start(f32[3,128]{1,0:T(4,128)S(1)} %add.18), channel_id=1, source_target_pairs={{0,11},{1,10},{2,9},{3,8},{4,15},{5,14},{6,13},{7,12},{8,3},{9,2},... | collective-permute-start | bytes 4616 | tf_op jit(solution)/shard_map/ppermute | solution.py:242
  19.0 2.1 %collective-permute-start.11 = (f32[3,128]{1,0:T(4,128)S(1)}, f32[3,128]{1,0:T(4,128)S(1)}, u32[]{:S(2)}, u32[]{:S(2)}) collective-permute-start(f32[3,128]{1,0:T(4,128)S(1)} %add.18), channel_id=1, source_target_pairs={{0,8},{1,9},{2,10},{3,11},{4,12},{5,13},{6,14},{7,15},{8,0},{9,1},... | collective-permute-start | bytes 4616 | tf_op jit(solution)/shard_map/ppermute | solution.py:242
  19.4 3.0 %collective-permute-start.8 = (f32[3,128]{1,0:T(4,128)S(1)}, f32[3,128]{1,0:T(4,128)S(1)}, u32[]{:S(2)}, u32[]{:S(2)}) collective-permute-start(f32[3,128]{1,0:T(4,128)S(1)} %add.18), channel_id=1, source_target_pairs={{0,9},{1,11},{2,8},{3,10},{4,13},{5,15},{6,12},{7,14},{8,1},{9,3},... | collective-permute-start | bytes 4616 | tf_op jit(solution)/shard_map/ppermute | solution.py:242
  19.7 3.0 %collective-permute-start.9 = (f32[3,128]{1,0:T(4,128)S(1)}, f32[3,128]{1,0:T(4,128)S(1)}, u32[]{:S(2)}, u32[]{:S(2)}) collective-permute-start(f32[3,128]{1,0:T(4,128)S(1)} %add.18), channel_id=1, source_target_pairs={{0,10},{1,8},{2,11},{3,9},{4,14},{5,12},{6,15},{7,13},{8,2},{9,0},... | collective-permute-start | bytes 4616 | tf_op jit(solution)/shard_map/ppermute | solution.py:242

commit v2 on v1

--- a/solution.py
+++ b/solution.py
@@ -108,9 +108,10 @@
             squared = jnp.dot(chosen, right, preferred_element_type=jnp.float32)
             scale = scale_ref[...]
             total = total + (jnp.exp2(squared[:, :objects] * scale) + jnp.exp2(squared[:, objects:] * scale))
+    parts = jnp.concatenate([part.astype(jnp.bfloat16) for part in thirds(total)], axis=1)
     return lax.dot_general(
-        jnp.ones((8, objects), jnp.float32), total, (((1,), (1,)), ((), ())),
-        precision=lax.Precision.HIGHEST, preferred_element_type=jnp.float32,
+        jnp.ones((8, parts.shape[1]), jnp.bfloat16), parts, (((1,), (1,)), ((), ())),
+        preferred_element_type=jnp.float32,
     )
 
 

time: 23.4 us -> 23 us (0.983)
  Pallas kernels: 6.39 us -> 5.81 us
    pallas_call x3, Pallas kernels: 5.05 us -> 4.46 us  [pair_side(): pl.pallas_call(functools.partial(pair_kernel, place), out_shape=jax.Shape...]
  transfers between devices with their start and end apart: 12 -> 12, of which waited for: 4 -> 4; matrix products, arithmetic and copies ran while one was open for 0% -> 0% of each run, Pallas kernels for 20% -> 19%
where the time goes in v2:
time: 23 us; the launch traced here: 22.9 us
  starting transfers between devices  11.2 us (49%)
  Pallas kernels  5.81 us (25%)
  waiting for transfers between devices  5.02 us (22%)
  other arithmetic  0.59 us (3%)
    ppermute x6, starting transfers between devices, moved(): return lax.ppermute(array, ('plane', 'tm'), pairs)  7.11 us
    pallas_call x3, Pallas kernels, pair_side(): pl.pallas_call(functools.partial(pair_kernel, place), out_shape=jax.Shape...  4.46 us
    ppermute x6, starting transfers between devices, taken(): return lax.ppermute(value, 'plane', move)  4.12 us
    ppermute x6, waiting for transfers between devices, moved(): return lax.ppermute(array, ('plane', 'tm'), pairs)  2.7 us
    ppermute x6, waiting for transfers between devices, taken(): return lax.ppermute(value, 'plane', move)  2.33 us
    pallas_call x1, Pallas kernels, own_side(): pl.pallas_call(functools.partial(own_kernel, places_of, factor), out_shap...  1.35 us
    add x1, other arithmetic, local(): sum((weight[place] * sums[place:place + 1] for place in range(weight.shap...  0.59 us
  transfers between devices with their start and end apart: 12, of which 4 were waited for; matrix products, arithmetic and copies ran while one was open for 0% of the time, Pallas kernels for 19%

profile of v2, /device:TPU:0, one launch (start us, length us, event | category | flops | bytes accessed | tf_op | source)
XLA Modules:
  0.0 22.9 jit_solution(14680131356710773493)
XLA Ops:
  0.0 0.0 copy-start
  0.0 0.5 %collective-permute-start = (f32[4,3,16,128]{3,2,1,0:T(8,128)}, f32[4,3,16,128]{3,2,1,0:T(8,128)S(1)}, u32[]{:S(2)}, u32[]{:S(2)}) collective-permute-start(f32[4,3,16,128]{3,2,1,0:T(8,128)} %coeffs_hbm.1), channel_id=1, source_target_pairs={{0,8},{8,0},{16,24},{24,16},{1,9},{9,1},{17,25},{25,17},{2,10},{10... | collective-permute-start | bytes 294920 | tf_op jit(solution)/shard_map/ppermute | solution.py:261
  0.5 0.2 copy-done
  0.7 0.5 %collective-permute-start.3 = (f32[1,128]{1,0:T(1,128)S(1)}, f32[1,128]{1,0:T(1,128)S(1)}, u32[]{:S(2)}, u32[]{:S(2)}) collective-permute-start(f32[1,128]{1,0:T(1,128)S(1)} %bitcast.22), channel_id=1, source_target_pairs={{0,8},{8,0},{16,24},{24,16},{1,9},{9,1},{17,25},{25,17},{2,10},{10... | collective-permute-start | bytes 1544 | tf_op jit(solution)/shard_map/ppermute | solution.py:261
  1.1 2.6 %collective-permute-start.2 = (f32[1,128]{1,0:T(1,128)S(1)}, f32[1,128]{1,0:T(1,128)S(1)}, u32[]{:S(2)}, u32[]{:S(2)}) collective-permute-start(f32[1,128]{1,0:T(1,128)S(1)} %bitcast.23), channel_id=1, source_target_pairs={{0,24},{8,16},{16,8},{24,0},{1,25},{9,17},{17,9},{25,1},{2,26},{10... | collective-permute-start | bytes 1544 | tf_op jit(solution)/shard_map/ppermute | solution.py:261
  3.7 0.0 collective-permute-start.1
  3.8 0.0 collective-permute-done.near_ref
  3.8 1.3 %own_side.1 = (f32[3,4,128]{2,1,0:T(4,128)S(1)}, bf16[16,128,128]{2,1,0:T(8,128)(2,1)S(1)}, f32[128,128]{1,0:T(8,128)S(1)}, bf16[32,96]{1,0:T(8,128)(2,1)S(1)}, bf16[16,128,128]{2,1,0:T(8,128)(2,1)S(1)}) custom-call(f32[4,3,16,128]{3,2,1,0:T(8,128)} %coeffs_hbm.1, s32[1,4]{1,0:T(1,128)} %bitcast.25, f32[1,128]{1,0:T(1,128)S(1)} %bitcast.24, ...), custom_call_target="tpu_custom_call" | custom-call | flops 10000000 | bytes 1000000 | tf_op jit(solution)/shard_map/own_side/pallas_call | solution.py:158
  5.1 0.0 collective-permute-done.3.radius_ref
  5.1 1.4 %pair_side.3.refs_0_ = f32[3,128]{1,0:T(4,128)S(1)} custom-call(bf16[32,96]{1,0:T(8,128)(2,1)S(1)} %get-tuple-element.14.basis_ref, bf16[16,128,128]{2,1,0:T(8,128)(2,1)S(1)} %get-tuple-element.15.left_ref, f32[128,128]{1,0:T(8,128)S(1)} %get-tuple-element.16.spread_ref, bf16[16,128,128]{2,1,0:T(8,128)(2,1)S(1)} %get-tuple-element.17.coeffs_ref, ...), custom_call_target="tpu_custom_call" | custom-call | flops 1073741824 | bytes 4000000 | tf_op jit(solution)/shard_map/pair_side/pallas_call | solution.py:189
  6.6 0.0 collective-permute-done.2.radius_ref
  6.6 2.3 %collective-permute-done.1.coeffs_ref = f32[4,3,16,128]{3,2,1,0:T(8,128)S(1)} collective-permute-done((f32[4,3,16,128]{3,2,1,0:T(8,128)}, f32[4,3,16,128]{3,2,1,0:T(8,128)S(1)}, u32[]{:S(2)}, u32[]{:S(2)}) %collective-permute-start.1) | collective-permute-done | bytes 98336 | tf_op jit(solution)/shard_map/ppermute | solution.py:261
  8.9 0.1 collective-permute-start.4
  9.0 0.4 %collective-permute-start.5 = (f32[1,128]{1,0:T(1,128)S(1)}, f32[1,128]{1,0:T(1,128)S(1)}, u32[]{:S(2)}, u32[]{:S(2)}) collective-permute-start(f32[1,128]{1,0:T(1,128)S(1)} %collective-permute-done.2.radius_ref), channel_id=1, source_target_pairs={{0,8},{8,0},{16,24},{24,16},{1,9},{9,1},{17,25},{25,17},{2,10},{10... | collective-permute-start | bytes 1544 | tf_op jit(solution)/shard_map/ppermute | solution.py:261
  9.4 1.5 %pair_side.4.refs_0_ = f32[3,128]{1,0:T(4,128)S(1)} custom-call(bf16[32,96]{1,0:T(8,128)(2,1)S(1)} %get-tuple-element.14.basis_ref, bf16[16,128,128]{2,1,0:T(8,128)(2,1)S(1)} %get-tuple-element.15.left_ref, f32[128,128]{1,0:T(8,128)S(1)} %get-tuple-element.16.spread_ref, f32[4,3,16,128]{3,2,1,0:T(8,128)S(1)} %collective-permute-done.1.coeffs_ref, ...), custom_call_target="tpu_custom_call" | custom-call | flops 1073741824 | bytes 4000000 | tf_op jit(solution)/shard_map/pair_side/pallas_call | solution.py:189
  10.9 0.0 collective-permute-done.5.radius_ref
  10.9 0.0 collective-permute-done.4.coeffs_ref
  10.9 1.5 %pair_side.5 = f32[3,128]{1,0:T(4,128)S(1)} custom-call(bf16[32,96]{1,0:T(8,128)(2,1)S(1)} %get-tuple-element.14.basis_ref, bf16[16,128,128]{2,1,0:T(8,128)(2,1)S(1)} %get-tuple-element.15.left_ref, f32[128,128]{1,0:T(8,128)S(1)} %get-tuple-element.16.spread_ref, f32[4,3,16,128]{3,2,1,0:T(8,128)S(1)} %collective-permute-done.4.coeffs_ref, ...), custom_call_target="tpu_custom_call" | custom-call | flops 1073741824 | bytes 4000000 | tf_op jit(solution)/shard_map/pair_side/pallas_call | solution.py:189
  12.5 2.3 %collective-permute-start.6 = (f32[3,128]{1,0:T(4,128)S(1)}, f32[3,128]{1,0:T(4,128)S(1)}, u32[]{:S(2)}, u32[]{:S(2)}) collective-permute-start(f32[3,128]{1,0:T(4,128)S(1)} %pair_side.5), channel_id=1, source_target_pairs={{0,12},{1,13},{2,14},{3,15},{4,8},{5,9},{6,10},{7,11},{8,4},{9,5},... | collective-permute-start | bytes 4616 | tf_op jit(solution)/shard_map/ppermute | solution.py:243
  14.8 0.4 %collective-permute-start.7 = (f32[3,128]{1,0:T(4,128)S(1)}, f32[3,128]{1,0:T(4,128)S(1)}, u32[]{:S(2)}, u32[]{:S(2)}) collective-permute-start(f32[3,128]{1,0:T(4,128)S(1)} %pair_side.5), channel_id=1, source_target_pairs={{0,8},{1,9},{2,10},{3,11},{4,12},{5,13},{6,14},{7,15},{8,0},{9,1},... | collective-permute-start | bytes 4616 | tf_op jit(solution)/shard_map/ppermute | solution.py:243
  15.2 1.2 %collective-permute-done.6 = f32[3,128]{1,0:T(4,128)S(1)} collective-permute-done((f32[3,128]{1,0:T(4,128)S(1)}, f32[3,128]{1,0:T(4,128)S(1)}, u32[]{:S(2)}, u32[]{:S(2)}) %collective-permute-start.6) | collective-permute-done | bytes 1568 | tf_op jit(solution)/shard_map/ppermute | solution.py:243
  16.4 0.0 collective-permute-done.7
  16.4 2.3 %collective-permute-start.10 = (f32[3,128]{1,0:T(4,128)S(1)}, f32[3,128]{1,0:T(4,128)S(1)}, u32[]{:S(2)}, u32[]{:S(2)}) collective-permute-start(f32[3,128]{1,0:T(4,128)S(1)} %add.18), channel_id=1, source_target_pairs={{0,11},{1,10},{2,9},{3,8},{4,15},{5,14},{6,13},{7,12},{8,3},{9,2},... | collective-permute-start | bytes 4616 | tf_op jit(solution)/shard_map/ppermute | solution.py:243
  18.6 0.4 %collective-permute-start.11 = (f32[3,128]{1,0:T(4,128)S(1)}, f32[3,128]{1,0:T(4,128)S(1)}, u32[]{:S(2)}, u32[]{:S(2)}) collective-permute-start(f32[3,128]{1,0:T(4,128)S(1)} %add.18), channel_id=1, source_target_pairs={{0,8},{1,9},{2,10},{3,11},{4,12},{5,13},{6,14},{7,15},{8,0},{9,1},... | collective-permute-start | bytes 4616 | tf_op jit(solution)/shard_map/ppermute | solution.py:243
  19.0 0.2 collective-permute-start.8
  19.3 1.5 %collective-permute-start.9 = (f32[3,128]{1,0:T(4,128)S(1)}, f32[3,128]{1,0:T(4,128)S(1)}, u32[]{:S(2)}, u32[]{:S(2)}) collective-permute-start(f32[3,128]{1,0:T(4,128)S(1)} %add.18), channel_id=1, source_target_pairs={{0,10},{1,8},{2,11},{3,9},{4,14},{5,12},{6,15},{7,13},{8,2},{9,0},... | collective-permute-start | bytes 4616 | tf_op jit(solution)/shard_map/ppermute | solution.py:243
  20.8 0.0 collective-permute-done.10
  20.8 0.0 collective-permute-done.11
  20.8 1.3 %collective-permute-done.8 = f32[3,128]{1,0:T(4,128)S(1)} collective-permute-done((f32[3,128]{1,0:T(4,128)S(1)}, f32[3,128]{1,0:T(4,128)S(1)}, u32[]{:S(2)}, u32[]{:S(2)}) %collective-permute-start.8) | collective-permute-done | bytes 1568 | tf_op jit(solution)/shard_map/ppermute | solution.py:243
  22.0 0.2 collective-permute-done.9
  22.3 0.6 %fusion = f32[4,128]{1,0:T(4,128)} fusion(f32[3,4,128]{2,1,0:T(4,128)S(1)} %get-tuple-element.13, f32[128]{0:T(128)S(1)} %get-tuple-element.22, f32[128]{0:T(128)S(1)} %get-tuple-element.23, f32[128]{0:T(128)S(1)} %get-tuple-element.21), kind=kLoop, calls=%fused_computation.1 | loop fusion | flops 2560 | bytes 9728 | tf_op jit(solution)/shard_map/add | solution.py:288
  (3 shorter events, 0.0 us)
Async XLA Ops:
  0.0 0.7 %copy-start = (f32[128]{0:T(128)S(1)}, f32[128]{0:T(128)}, u32[]{:S(2)}) copy-start(f32[128]{0:T(128)} %param.4) | copy-start | bytes 1540
  0.0 3.8 %collective-permute-start = (f32[4,3,16,128]{3,2,1,0:T(8,128)}, f32[4,3,16,128]{3,2,1,0:T(8,128)S(1)}, u32[]{:S(2)}, u32[]{:S(2)}) collective-permute-start(f32[4,3,16,128]{3,2,1,0:T(8,128)} %coeffs_hbm.1), channel_id=1, source_target_pairs={{0,8},{8,0},{16,24},{24,16},{1,9},{9,1},{17,25},{25,17},{2,10},{10... | collective-permute-start | bytes 294920 | tf_op jit(solution)/shard_map/ppermute | solution.py:261
  0.7 4.5 %collective-permute-start.3 = (f32[1,128]{1,0:T(1,128)S(1)}, f32[1,128]{1,0:T(1,128)S(1)}, u32[]{:S(2)}, u32[]{:S(2)}) collective-permute-start(f32[1,128]{1,0:T(1,128)S(1)} %bitcast.22), channel_id=1, source_target_pairs={{0,8},{8,0},{16,24},{24,16},{1,9},{9,1},{17,25},{25,17},{2,10},{10... | collective-permute-start | bytes 1544 | tf_op jit(solution)/shard_map/ppermute | solution.py:261
  1.1 5.4 %collective-permute-start.2 = (f32[1,128]{1,0:T(1,128)S(1)}, f32[1,128]{1,0:T(1,128)S(1)}, u32[]{:S(2)}, u32[]{:S(2)}) collective-permute-start(f32[1,128]{1,0:T(1,128)S(1)} %bitcast.23), channel_id=1, source_target_pairs={{0,24},{8,16},{16,8},{24,0},{1,25},{9,17},{17,9},{25,1},{2,26},{10... | collective-permute-start | bytes 1544 | tf_op jit(solution)/shard_map/ppermute | solution.py:261
  3.7 5.1 %collective-permute-start.1 = (f32[4,3,16,128]{3,2,1,0:T(8,128)}, f32[4,3,16,128]{3,2,1,0:T(8,128)S(1)}, u32[]{:S(2)}, u32[]{:S(2)}) collective-permute-start(f32[4,3,16,128]{3,2,1,0:T(8,128)} %coeffs_hbm.1), channel_id=1, source_target_pairs={{0,24},{8,16},{16,8},{24,0},{1,25},{9,17},{17,9},{25,1},{2,26},{10... | collective-permute-start | bytes 294920 | tf_op jit(solution)/shard_map/ppermute | solution.py:261
  8.9 2.1 %collective-permute-start.4 = (f32[4,3,16,128]{3,2,1,0:T(8,128)S(1)}, f32[4,3,16,128]{3,2,1,0:T(8,128)S(1)}, u32[]{:S(2)}, u32[]{:S(2)}) collective-permute-start(f32[4,3,16,128]{3,2,1,0:T(8,128)S(1)} %collective-permute-done.1.coeffs_ref), channel_id=1, source_target_pairs={{0,8},{8,0},{16,24},{24,16},{1,9},{9,1},{17,25},{25,17},{2,10},{10... | collective-permute-start | bytes 294920 | tf_op jit(solution)/shard_map/ppermute | solution.py:261
  9.0 1.9 %collective-permute-start.5 = (f32[1,128]{1,0:T(1,128)S(1)}, f32[1,128]{1,0:T(1,128)S(1)}, u32[]{:S(2)}, u32[]{:S(2)}) collective-permute-start(f32[1,128]{1,0:T(1,128)S(1)} %collective-permute-done.2.radius_ref), channel_id=1, source_target_pairs={{0,8},{8,0},{16,24},{24,16},{1,9},{9,1},{17,25},{25,17},{2,10},{10... | collective-permute-start | bytes 1544 | tf_op jit(solution)/shard_map/ppermute | solution.py:261
  12.5 3.9 %collective-permute-start.6 = (f32[3,128]{1,0:T(4,128)S(1)}, f32[3,128]{1,0:T(4,128)S(1)}, u32[]{:S(2)}, u32[]{:S(2)}) collective-permute-start(f32[3,128]{1,0:T(4,128)S(1)} %pair_side.5), channel_id=1, source_target_pairs={{0,12},{1,13},{2,14},{3,15},{4,8},{5,9},{6,10},{7,11},{8,4},{9,5},... | collective-permute-start | bytes 4616 | tf_op jit(solution)/shard_map/ppermute | solution.py:243
  14.8 1.6 %collective-permute-start.7 = (f32[3,128]{1,0:T(4,128)S(1)}, f32[3,128]{1,0:T(4,128)S(1)}, u32[]{:S(2)}, u32[]{:S(2)}) collective-permute-start(f32[3,128]{1,0:T(4,128)S(1)} %pair_side.5), channel_id=1, source_target_pairs={{0,8},{1,9},{2,10},{3,11},{4,12},{5,13},{6,14},{7,15},{8,0},{9,1},... | collective-permute-start | bytes 4616 | tf_op jit(solution)/shard_map/ppermute | solution.py:243
  16.4 4.4 %collective-permute-start.10 = (f32[3,128]{1,0:T(4,128)S(1)}, f32[3,128]{1,0:T(4,128)S(1)}, u32[]{:S(2)}, u32[]{:S(2)}) collective-permute-start(f32[3,128]{1,0:T(4,128)S(1)} %add.18), channel_id=1, source_target_pairs={{0,11},{1,10},{2,9},{3,8},{4,15},{5,14},{6,13},{7,12},{8,3},{9,2},... | collective-permute-start | bytes 4616 | tf_op jit(solution)/shard_map/ppermute | solution.py:243
  18.6 2.1 %collective-permute-start.11 = (f32[3,128]{1,0:T(4,128)S(1)}, f32[3,128]{1,0:T(4,128)S(1)}, u32[]{:S(2)}, u32[]{:S(2)}) collective-permute-start(f32[3,128]{1,0:T(4,128)S(1)} %add.18), channel_id=1, source_target_pairs={{0,8},{1,9},{2,10},{3,11},{4,12},{5,13},{6,14},{7,15},{8,0},{9,1},... | collective-permute-start | bytes 4616 | tf_op jit(solution)/shard_map/ppermute | solution.py:243
  19.0 3.0 %collective-permute-start.8 = (f32[3,128]{1,0:T(4,128)S(1)}, f32[3,128]{1,0:T(4,128)S(1)}, u32[]{:S(2)}, u32[]{:S(2)}) collective-permute-start(f32[3,128]{1,0:T(4,128)S(1)} %add.18), channel_id=1, source_target_pairs={{0,9},{1,11},{2,8},{3,10},{4,13},{5,15},{6,12},{7,14},{8,1},{9,3},... | collective-permute-start | bytes 4616 | tf_op jit(solution)/shard_map/ppermute | solution.py:243
  19.3 3.0 %collective-permute-start.9 = (f32[3,128]{1,0:T(4,128)S(1)}, f32[3,128]{1,0:T(4,128)S(1)}, u32[]{:S(2)}, u32[]{:S(2)}) collective-permute-start(f32[3,128]{1,0:T(4,128)S(1)} %add.18), channel_id=1, source_target_pairs={{0,10},{1,8},{2,11},{3,9},{4,14},{5,12},{6,15},{7,13},{8,2},{9,0},... | collective-permute-start | bytes 4616 | tf_op jit(solution)/shard_map/ppermute | solution.py:243
